TPU v7x, 256 devices: a whole 4x4x8 slice. The times are simulated.
256 devices in a mesh: ka: 32 (over y_hi, z, core), rad: 8 (over y_lo, x).
Axes of the slice: x: 4, y: 4 (y_hi: 2, y_lo: 2; y = y_hi * 2 + y_lo), z: 8, core: 2. Of those that a mesh axis runs over, the one named last changes fastest.
Arguments:
- prev_wave: float32 [32, 192, 64, 128], P('ka', None, 'rad'), may hold values from -6 to 6
- cur_wave: float32 [32, 192, 64, 128], P('ka', None, 'rad'), may hold values from -6 to 6
- legendre: float32 [32, 192, 192], P('ka'), may hold values from -0.4375 to 0.4375
- potential: float32 [192, 64, 128], P(None, 'rad'), may hold values from -0.15 to 0.15
- radial: float32 [3, 64], P(None, 'rad'), may hold values from 0.02 to 0.3
- rot_const: float32 [128], replicated, may hold values from 0.05 to 0.5
- first_row: int32 [32], P('ka'), may hold values from 0 to 96, as said below
Outputs:
- prev_out: float32 [32, 192, 64, 128], P('ka', None, 'rad')
- cur_out: float32 [32, 192, 64, 128], P('ka', None, 'rad')
Inputs may be any that keep to these rules, and one draw needn't show every extreme that they name: first_row never falls with K, first_row[0] = 0 and first_row[31] = 96.
All inputs are finite; a program needn't handle non-finite values.
Results may differ from a plain program's by a relative error of at most 0.0003.
Values sent between devices are 32-bit elements; how exact they have to be, the bound alone decides.
No kernel may reach another device: no remote copies, remote signals or barrier semaphores. Data moves between devices by JAX's collectives and lax.ppermute only.
A program may use at most 64 MiB of HBM per device.

v0:
```python
import functools
import math

import jax
import jax.numpy as jnp
from jax import lax
from jax.experimental import pallas as pl
from jax.experimental.pallas import tpu as pltpu
from jax.sharding import PartitionSpec as P


STEPS = 4
KICKS = 2

COEF = 0.1
RKIN = 0.04
EMID = 0.75

VMEM = pl.BlockSpec(memory_space=pltpu.VMEM)
SMEM = pl.BlockSpec(memory_space=pltpu.SMEM)
PARAMS = pltpu.CompilerParams(vmem_limit_bytes=16 << 20)


def both_ways(pairs):
    return [(a, b) for a, b in pairs] + [(b, a) for a, b in pairs]


def pairings(nka, nrad):
    at = lambda k, r: k * nrad + r
    k_even = [(at(k, r), at(k + 1, r)) for k in range(0, nka, 2) for r in range(nrad)]
    k_odd = [(at(k, r), at(k + 1, r)) for k in range(1, nka - 1, 2) for r in range(nrad)]
    k_odd += [(at(k, r), at(k, r + 1)) for k in (0, nka - 1) for r in range(0, nrad, 2)]
    r_even = [(at(k, r), at(k, r + 1)) for k in range(nka) for r in range(0, nrad, 2)]
    r_odd = [(at(k, r), at(k, r + 1)) for k in range(nka) for r in range(1, nrad - 1, 2)]
    r_odd += [(at(k, r), at(k + 1, r)) for k in range(0, nka, 2) for r in (0, nrad - 1)]
    return [both_ways(p) for p in (k_even, k_odd, r_even, r_odd)]


def split(x):
    high = x.astype(jnp.bfloat16)
    return high, (x - high.astype(jnp.float32)).astype(jnp.bfloat16)


def mul(a, b):
    return jnp.dot(a, b, preferred_element_type=jnp.float32)


def groups(rows):
    quarter = rows // 4
    inside = list(range(quarter, rows - quarter))
    return inside, [n for n in range(rows) if n not in inside]


def fade_row(rows, n):
    return rows + n


def couple_row(rows, n):
    return 2 * rows + n


def centri_row(rows, n):
    return 3 * rows + n


def halo_row(rows, n):
    return 4 * rows + n


def strided(rows, n, nrot):
    return pl.ds(n, nrot, stride=rows)


def at_row(table, n):
    return table[n : n + 1, :]


def setup_kernel(rows, nka, nrad, where, radial, legendre, rot, *outs):
    scal, th, tl, bh, bl, kin2, rotq, qp, s_in, s_out, live = outs
    kpos, rpos, first = where[0], where[1], where[2]
    nrot, width = rotq.shape
    jtop = nka - 1
    kodd, rodd = kpos % 2, rpos % 2
    row = lambda value: jnp.full((1, width), value, jnp.float32)
    for n in range(rows):
        damp = jnp.exp(-row(radial[2, n]))
        put = lambda at, value: scal.__setitem__((pl.ds(at, 1), slice(None)), value)
        put(n, 2.0 * damp)
        put(fade_row(rows, n), damp * damp)
        put(couple_row(rows, n), 2.0 * damp * radial[1, n])
        put(centri_row(rows, n), row(radial[0, n]))
        if n in (0, rows - 1):
            edge = 0 if n == 0 else nrad - 1
            share = jnp.where(rpos == edge, 0.0, 2.0 * COEF * damp)
            from_even = (rodd == 1) if n == 0 else (rodd == 0)
            base = 0 if n == 0 else 2
            put(halo_row(rows, base), jnp.where(from_even, share, 0.0))
            put(halo_row(rows, base + 1), jnp.where(from_even, 0.0, share))
    put(halo_row(rows, 4), row(rodd.astype(jnp.float32)))
    j = lax.broadcasted_iota(jnp.int32, (nrot, width), 0)
    alive = (j >= first).astype(jnp.float32)
    live[...] = alive
    norm = nrot * (nrot + 1)
    qrot = (j * (j + 1)).astype(jnp.float32) / norm
    rotq[...] = rot[...] * qrot
    qp[...] = qrot + (jtop * (jtop + 1) - 2 * kpos * kpos).astype(jnp.float32) / norm

    def coupling(k):
        a = jnp.maximum(j * (j + 1) - k * (k + 1), 0)
        b = jnp.maximum(jtop * (jtop + 1) - k * (k + 1), 0)
        return alive * (jnp.sqrt((a * b).astype(jnp.float32)) / (nrot * nka))

    outer_k = kpos - 1 + kodd
    s_in[...] = coupling(kpos - kodd)
    s_out[...] = jnp.where(outer_k < 0, 0.0, coupling(outer_k))
    transform = legendre[0]
    th[...], tl[...] = split(transform.T)
    keep = lax.broadcasted_iota(jnp.int32, transform.shape, 0) >= first
    bh[...], bl[...] = split(jnp.where(keep, transform, 0.0))
    differ = lax.broadcasted_iota(jnp.int32, (width, width), 0) - lax.broadcasted_iota(
        jnp.int32, (width, width), 1
    )
    parity = (1 - 2 * (jnp.abs(differ) & 1)).astype(jnp.float32)
    square = jnp.maximum(differ * differ, 1).astype(jnp.float32)
    sinc = jnp.where(differ == 0, jnp.float32(math.pi * math.pi / 3.0), 2.0 * parity / square)
    kh, kl = split(RKIN * sinc)
    kin2[...] = jnp.concatenate(
        [
            jnp.concatenate([kh, kl], axis=1),
            jnp.concatenate([kh, jnp.zeros_like(kl)], axis=1),
        ],
        axis=0,
    )


def start_kernel(rows, where, wave, first_group, second_group, whole, send_even, send_odd):
    nrot, width = send_even.shape
    inside, outside = groups(rows)
    alive = lax.broadcasted_iota(jnp.int32, (nrot, width), 0) >= where[2]
    for n in range(rows):
        v = jnp.where(alive, wave[strided(rows, n, nrot), :], 0.0)
        whole[n] = v
        if n in inside:
            first_group[inside.index(n)] = v
        else:
            second_group[outside.index(n)] = v
    odd = where[1] % 2 == 1
    low, high = whole[0], whole[rows - 1]
    send_even[...] = jnp.where(odd, low, high)
    send_odd[...] = jnp.where(odd, high, low)


def local_kernel(rows, opening, scal, cur, prev, pot, th, tl, bh, bl, kin2, rotq, qp, live, out):
    nrot, width = rotq.shape
    for i in range(0, rows, 2):
        x = [cur[i], cur[i + 1]]
        xh, xl = split(jnp.concatenate(x, axis=1))
        angular = mul(th[...], xh) + mul(tl[...], xh) + mul(th[...], xl)
        y = jnp.concatenate([pot[strided(rows, i + h, nrot), :] for h in range(2)], axis=1) * angular
        yh, yl = split(y)
        back = mul(bh[...], yh) + mul(bl[...], yh) + mul(bh[...], yl)
        for h in range(2):
            n = i + h
            part = slice(h * width, (h + 1) * width)
            both = mul(jnp.concatenate([xh[:, part], xl[:, part]], axis=1), kin2[...])
            total = back[:, part] + (both[:, :width] + both[:, width:])
            diag = rotq[...] + (
                at_row(scal, centri_row(rows, n)) * qp[...] + (2.0 * COEF - EMID)
            )
            near = [cur[o] for o in (n - 1, n + 1) if 0 <= o < rows]
            total = total + diag * x[h] - COEF * sum(near[1:], near[0])
            past = live[...] * prev[strided(rows, n, nrot), :] if opening else prev[n]
            out[n] = at_row(scal, n) * total - at_row(scal, fade_row(rows, n)) * past


def plane(rows, n, scal, local, inner, outer, s_in, s_out, halos):
    new = local[n] + at_row(scal, couple_row(rows, n)) * (
        s_in[...] * inner[n] + s_out[...] * outer
    )
    for edge, base in ((0, 0), (rows - 1, 2)):
        if n == edge:
            new = new - (
                at_row(scal, halo_row(rows, base)) * halos[0][...]
                + at_row(scal, halo_row(rows, base + 1)) * halos[1][...]
            )
    return new


def inside_kernel(rows, scal, local, inner, outer, s_in, s_out, out):
    inside, _ = groups(rows)
    for i, n in enumerate(inside):
        out[i] = plane(rows, n, scal, local, inner, outer[i], s_in, s_out, None)


def outside_kernel(rows, scal, local, inner, outer, s_in, s_out, got_even, got_odd, done, *outs):
    out, whole, send_even, send_odd = outs
    inside, outside = groups(rows)
    for i, n in enumerate(outside):
        v = plane(rows, n, scal, local, inner, outer[i], s_in, s_out, (got_even, got_odd))
        out[i] = v
        whole[n] = v
    low, high = whole[0], whole[rows - 1]
    odd = at_row(scal, halo_row(rows, 4)) > 0.5
    send_even[...] = jnp.where(odd, low, high)
    send_odd[...] = jnp.where(odd, high, low)
    for i, n in enumerate(inside):
        whole[n] = done[i]


def finish_kernel(rows, scal, local, inner, outer_a, outer_b, s_in, s_out, got_even, got_odd, out):
    nrot, _ = s_in.shape
    for outer, members in zip((outer_a, outer_b), groups(rows)):
        for i, n in enumerate(members):
            out[strided(rows, n, nrot), :] = plane(
                rows, n, scal, local, inner, outer[i], s_in, s_out, (got_even, got_odd)
            )


def turn_kernel(rows, wave, out):
    for n in range(rows):
        out[strided(rows, n, wave.shape[1]), :] = wave[n]


def on_device(prev_wave, cur_wave, legendre, potential, radial, rot_const, first_row):
    axes = ("ka", "rad")
    nka, nrad = lax.axis_size("ka"), lax.axis_size("rad")
    k_even, k_odd, r_even, r_odd = pairings(nka, nrad)
    nrot, rows, width = cur_wave.shape[1:]
    where = jnp.stack([lax.axis_index("ka"), lax.axis_index("rad"), first_row[0]]).astype(jnp.int32)
    flat = (nrot * rows, width)
    f32 = lambda *shape: jax.ShapeDtypeStruct(shape, jnp.float32)
    b16 = lambda *shape: jax.ShapeDtypeStruct(shape, jnp.bfloat16)
    face, block = f32(nrot, width), f32(rows, nrot, width)
    inside, outside = groups(rows)
    part_a, part_b = f32(len(inside), nrot, width), f32(len(outside), nrot, width)

    def call(kernel, ins, outs, *static):
        return pl.pallas_call(
            functools.partial(kernel, rows, *static),
            out_shape=outs,
            in_specs=ins,
            out_specs=jax.tree.map(lambda _: VMEM, outs),
            compiler_params=PARAMS,
        )

    setup = call(
        setup_kernel,
        [SMEM, SMEM, VMEM, VMEM],
        [
            f32(4 * rows + 8, width),
            b16(nrot, nrot),
            b16(nrot, nrot),
            b16(nrot, nrot),
            b16(nrot, nrot),
            b16(2 * width, 2 * width),
        ]
        + [face] * 5,
        nka,
        nrad,
    )
    start = call(start_kernel, [SMEM, VMEM], [part_a, part_b, block, face, face])
    local_call = [call(local_kernel, [VMEM] * 12, block, o) for o in (False, True)]
    inside_call = call(inside_kernel, [VMEM] * 6, part_a)
    outside_call = call(outside_kernel, [VMEM] * 9, [part_b, block, face, face])
    finish = call(finish_kernel, [VMEM] * 9, f32(*flat))
    turn_back = call(turn_kernel, [VMEM], f32(*flat))

    a, b, whole, send_even, send_odd = start(where, cur_wave.reshape(flat))
    prev = prev_wave.reshape(flat)
    pot = potential.reshape(flat)
    total = KICKS * STEPS
    for n in range(total):
        if n:
            a = inside_call(scal, local, inner, outer_a, s_in, s_out)
        new_outer_a = lax.ppermute(a, axes, k_odd)
        if n:
            b, made, send_even, send_odd = outside_call(
                scal, local, inner, outer_b, s_in, s_out, got_even, got_odd, a
            )
            prev, whole = whole, made
        outer_a = new_outer_a
        outer_b = lax.ppermute(b, axes, k_odd)
        got_odd = lax.ppermute(send_odd, axes, r_odd)
        got_even = lax.ppermute(send_even, axes, r_even)
        inner = lax.ppermute(whole, axes, k_even)
        if n == 0:
            scal, th, tl, bh, bl, kin2, rotq, qp, s_in, s_out, live = setup(
                where, radial, legendre, rot_const[None]
            )
        local = local_call[n == 0](scal, whole, prev, pot, th, tl, bh, bl, kin2, rotq, qp, live)
    prev_out = turn_back(whole)
    cur_out = finish(scal, local, inner, outer_a, outer_b, s_in, s_out, got_even, got_odd)
    shape = (1, nrot, rows, width)
    return (prev_out.reshape(shape), cur_out.reshape(shape))


def solution(mesh):
    placed = (
        P("ka", None, "rad", None),
        P("ka", None, "rad", None),
        P("ka", None, None),
        P(None, "rad", None),
        P(None, "rad"),
        P(),
        P("ka"),
    )
    return jax.shard_map(
        on_device,
        mesh=mesh,
        in_specs=placed,
        out_specs=(P("ka", None, "rad", None), P("ka", None, "rad", None)),
        check_vma=False,
    )
```

profile of v0, /device:TPU:16, one launch (start us, length us, event | category | flops | bytes accessed | tf_op | source)
XLA Modules:
  0.0 139.4 jit_solution(17668890617317188471)
XLA Ops:
  3.4 5.7 %collective-permute-start.4 = (f32[4,192,128]{2,1,0:T(8,128)S(1)}, f32[4,192,128]{2,1,0:T(8,128)S(1)}, u32[]{:S(2)}, u32[]{:S(2)}) collective-permute-start(f32[4,192,128]{2,1,0:T(8,128)S(1)} %get-tuple-element.61), channel_id=1, source_target_pairs={{8,16},{9,17},{10,18},{11,19},{12,20},{13,21},{14,22},{15,23},{24,... | collective-permute-start | bytes 1179656 | tf_op jit(solution)/shard_map/ppermute | solution.py:275
  9.2 1.5 %collective-permute-start.2 = (f32[192,128]{1,0:T(8,128)S(1)}, f32[192,128]{1,0:T(8,128)S(1)}, u32[]{:S(2)}, u32[]{:S(2)}) collective-permute-start(f32[192,128]{1,0:T(8,128)S(1)} %get-tuple-element.59), channel_id=1, source_target_pairs={{0,1},{2,3},{4,5},{6,7},{8,9},{10,11},{12,13},{14,15},{16,17},{18,... | collective-permute-start | bytes 294920 | tf_op jit(solution)/shard_map/ppermute | solution.py:284
  14.3 1.6 %shard_map.88.local = f32[8,192,128]{2,1,0:T(8,128)S(1)} custom-call(f32[40,128]{1,0:T(8,128)S(1)} %get-tuple-element.46.scal, f32[8,192,128]{2,1,0:T(8,128)S(1)} %get-tuple-element.47.cur.prev, f32[1536,128]{1,0:T(8,128)S(1)} %bitcast.17, f32[1536,128]{1,0:T(8,128)S(1)} %bitcast.8, bf16[192,192]{1,0:T(8,128)(2,1)S(1)} %get-tuple-element.48.th, ...), custom_call_target="tpu_custom_call" | custom-call | tf_op jit(solution)/shard_map/pallas_call | solution.py:290
  16.9 4.1 %collective-permute-done.1.outer = f32[4,192,128]{2,1,0:T(8,128)S(1)} collective-permute-done((f32[4,192,128]{2,1,0:T(8,128)S(1)}, f32[4,192,128]{2,1,0:T(8,128)S(1)}, u32[]{:S(2)}, u32[]{:S(2)}) %collective-permute-start.1) | collective-permute-done | bytes 393248 | tf_op jit(solution)/shard_map/ppermute | solution.py:282
  21.3 5.4 %collective-permute-start.9 = (f32[4,192,128]{2,1,0:T(8,128)S(1)}, f32[4,192,128]{2,1,0:T(8,128)S(1)}, u32[]{:S(2)}, u32[]{:S(2)}) collective-permute-start(f32[4,192,128]{2,1,0:T(8,128)S(1)} %shard_map.89.done), channel_id=1, source_target_pairs={{8,16},{9,17},{10,18},{11,19},{12,20},{13,21},{14,22},{15,23},{24,... | collective-permute-start | bytes 1179656 | tf_op jit(solution)/shard_map/ppermute | solution.py:275
  27.2 1.5 %shard_map.91.local = f32[8,192,128]{2,1,0:T(8,128)S(1)} custom-call(f32[40,128]{1,0:T(8,128)S(1)} %get-tuple-element.46.scal, f32[8,192,128]{2,1,0:T(8,128)S(1)} %get-tuple-element.62.cur.prev, f32[8,192,128]{2,1,0:T(8,128)S(1)} %get-tuple-element.47.cur.prev, f32[1536,128]{1,0:T(8,128)S(1)} %bitcast.9, bf16[192,192]{1,0:T(8,128)(2,1)S(1)} %get-tuple-element.48.th, ...), custom_call_target="tpu_custom_call" | custom-call | tf_op jit(solution)/shard_map/pallas_call | solution.py:290
  28.7 4.3 %collective-permute-done.9.outer = f32[4,192,128]{2,1,0:T(8,128)S(1)} collective-permute-done((f32[4,192,128]{2,1,0:T(8,128)S(1)}, f32[4,192,128]{2,1,0:T(8,128)S(1)}, u32[]{:S(2)}, u32[]{:S(2)}) %collective-permute-start.9) | collective-permute-done | bytes 393248 | tf_op jit(solution)/shard_map/ppermute | solution.py:275
  33.1 4.4 %collective-permute-done.6.outer = f32[4,192,128]{2,1,0:T(8,128)S(1)} collective-permute-done((f32[4,192,128]{2,1,0:T(8,128)S(1)}, f32[4,192,128]{2,1,0:T(8,128)S(1)}, u32[]{:S(2)}, u32[]{:S(2)}) %collective-permute-start.6) | collective-permute-done | bytes 393248 | tf_op jit(solution)/shard_map/ppermute | solution.py:282
  37.8 5.4 %collective-permute-start.14 = (f32[4,192,128]{2,1,0:T(8,128)S(1)}, f32[4,192,128]{2,1,0:T(8,128)S(1)}, u32[]{:S(2)}, u32[]{:S(2)}) collective-permute-start(f32[4,192,128]{2,1,0:T(8,128)S(1)} %shard_map.92.done), channel_id=1, source_target_pairs={{8,16},{9,17},{10,18},{11,19},{12,20},{13,21},{14,22},{15,23},{24,... | collective-permute-start | bytes 1179656 | tf_op jit(solution)/shard_map/ppermute | solution.py:275
  43.3 1.5 %shard_map.94.local = f32[8,192,128]{2,1,0:T(8,128)S(1)} custom-call(f32[40,128]{1,0:T(8,128)S(1)} %get-tuple-element.46.scal, f32[8,192,128]{2,1,0:T(8,128)S(1)} %get-tuple-element.66.cur.prev, f32[8,192,128]{2,1,0:T(8,128)S(1)} %get-tuple-element.62.cur.prev, f32[1536,128]{1,0:T(8,128)S(1)} %bitcast.10, bf16[192,192]{1,0:T(8,128)(2,1)S(1)} %get-tuple-element.48.th, ...), custom_call_target="tpu_custom_call" | custom-call | tf_op jit(solution)/shard_map/pallas_call | solution.py:290
  44.8 4.0 %collective-permute-done.14.outer = f32[4,192,128]{2,1,0:T(8,128)S(1)} collective-permute-done((f32[4,192,128]{2,1,0:T(8,128)S(1)}, f32[4,192,128]{2,1,0:T(8,128)S(1)}, u32[]{:S(2)}, u32[]{:S(2)}) %collective-permute-start.14) | collective-permute-done | bytes 393248 | tf_op jit(solution)/shard_map/ppermute | solution.py:275
  48.9 5.1 %collective-permute-done.11.outer = f32[4,192,128]{2,1,0:T(8,128)S(1)} collective-permute-done((f32[4,192,128]{2,1,0:T(8,128)S(1)}, f32[4,192,128]{2,1,0:T(8,128)S(1)}, u32[]{:S(2)}, u32[]{:S(2)}) %collective-permute-start.11) | collective-permute-done | bytes 393248 | tf_op jit(solution)/shard_map/ppermute | solution.py:282
  54.3 4.3 %collective-permute-start.19 = (f32[4,192,128]{2,1,0:T(8,128)S(1)}, f32[4,192,128]{2,1,0:T(8,128)S(1)}, u32[]{:S(2)}, u32[]{:S(2)}) collective-permute-start(f32[4,192,128]{2,1,0:T(8,128)S(1)} %shard_map.95.done), channel_id=1, source_target_pairs={{8,16},{9,17},{10,18},{11,19},{12,20},{13,21},{14,22},{15,23},{24,... | collective-permute-start | bytes 1179656 | tf_op jit(solution)/shard_map/ppermute | solution.py:275
  59.8 1.5 %shard_map.97.local = f32[8,192,128]{2,1,0:T(8,128)S(1)} custom-call(f32[40,128]{1,0:T(8,128)S(1)} %get-tuple-element.46.scal, f32[8,192,128]{2,1,0:T(8,128)S(1)} %get-tuple-element.70.cur.prev, f32[8,192,128]{2,1,0:T(8,128)S(1)} %get-tuple-element.66.cur.prev, f32[1536,128]{1,0:T(8,128)S(1)} %bitcast.11, bf16[192,192]{1,0:T(8,128)(2,1)S(1)} %get-tuple-element.48.th, ...), custom_call_target="tpu_custom_call" | custom-call | tf_op jit(solution)/shard_map/pallas_call | solution.py:290
  61.2 4.0 %collective-permute-done.19.outer = f32[4,192,128]{2,1,0:T(8,128)S(1)} collective-permute-done((f32[4,192,128]{2,1,0:T(8,128)S(1)}, f32[4,192,128]{2,1,0:T(8,128)S(1)}, u32[]{:S(2)}, u32[]{:S(2)}) %collective-permute-start.19) | collective-permute-done | bytes 393248 | tf_op jit(solution)/shard_map/ppermute | solution.py:275
  65.3 4.1 %collective-permute-done.16.outer = f32[4,192,128]{2,1,0:T(8,128)S(1)} collective-permute-done((f32[4,192,128]{2,1,0:T(8,128)S(1)}, f32[4,192,128]{2,1,0:T(8,128)S(1)}, u32[]{:S(2)}, u32[]{:S(2)}) %collective-permute-start.16) | collective-permute-done | bytes 393248 | tf_op jit(solution)/shard_map/ppermute | solution.py:282
  69.7 5.4 %collective-permute-start.24 = (f32[4,192,128]{2,1,0:T(8,128)S(1)}, f32[4,192,128]{2,1,0:T(8,128)S(1)}, u32[]{:S(2)}, u32[]{:S(2)}) collective-permute-start(f32[4,192,128]{2,1,0:T(8,128)S(1)} %shard_map.98.done), channel_id=1, source_target_pairs={{8,16},{9,17},{10,18},{11,19},{12,20},{13,21},{14,22},{15,23},{24,... | collective-permute-start | bytes 1179656 | tf_op jit(solution)/shard_map/ppermute | solution.py:275
  75.2 1.5 %shard_map.100.local = f32[8,192,128]{2,1,0:T(8,128)S(1)} custom-call(f32[40,128]{1,0:T(8,128)S(1)} %get-tuple-element.46.scal, f32[8,192,128]{2,1,0:T(8,128)S(1)} %get-tuple-element.74.cur.prev, f32[8,192,128]{2,1,0:T(8,128)S(1)} %get-tuple-element.70.cur.prev, f32[1536,128]{1,0:T(8,128)S(1)} %bitcast.12, bf16[192,192]{1,0:T(8,128)(2,1)S(1)} %get-tuple-element.48.th, ...), custom_call_target="tpu_custom_call" | custom-call | tf_op jit(solution)/shard_map/pallas_call | solution.py:290
  76.7 4.0 %collective-permute-done.24.outer = f32[4,192,128]{2,1,0:T(8,128)S(1)} collective-permute-done((f32[4,192,128]{2,1,0:T(8,128)S(1)}, f32[4,192,128]{2,1,0:T(8,128)S(1)}, u32[]{:S(2)}, u32[]{:S(2)}) %collective-permute-start.24) | collective-permute-done | bytes 393248 | tf_op jit(solution)/shard_map/ppermute | solution.py:275
  80.8 7.0 %collective-permute-done.21.outer = f32[4,192,128]{2,1,0:T(8,128)S(1)} collective-permute-done((f32[4,192,128]{2,1,0:T(8,128)S(1)}, f32[4,192,128]{2,1,0:T(8,128)S(1)}, u32[]{:S(2)}, u32[]{:S(2)}) %collective-permute-start.21) | collective-permute-done | bytes 393248 | tf_op jit(solution)/shard_map/ppermute | solution.py:282
  88.0 4.6 %collective-permute-start.29 = (f32[4,192,128]{2,1,0:T(8,128)S(1)}, f32[4,192,128]{2,1,0:T(8,128)S(1)}, u32[]{:S(2)}, u32[]{:S(2)}) collective-permute-start(f32[4,192,128]{2,1,0:T(8,128)S(1)} %shard_map.101.done), channel_id=1, source_target_pairs={{8,16},{9,17},{10,18},{11,19},{12,20},{13,21},{14,22},{15,23},{24,... | collective-permute-start | bytes 1179656 | tf_op jit(solution)/shard_map/ppermute | solution.py:275
  93.5 1.5 %shard_map.103.local = f32[8,192,128]{2,1,0:T(8,128)S(1)} custom-call(f32[40,128]{1,0:T(8,128)S(1)} %get-tuple-element.46.scal, f32[8,192,128]{2,1,0:T(8,128)S(1)} %get-tuple-element.78.cur.prev, f32[8,192,128]{2,1,0:T(8,128)S(1)} %get-tuple-element.74.cur.prev, f32[1536,128]{1,0:T(8,128)S(1)} %bitcast.13, bf16[192,192]{1,0:T(8,128)(2,1)S(1)} %get-tuple-element.48.th, ...), custom_call_target="tpu_custom_call" | custom-call | tf_op jit(solution)/shard_map/pallas_call | solution.py:290
  95.0 4.6 %collective-permute-done.29.outer = f32[4,192,128]{2,1,0:T(8,128)S(1)} collective-permute-done((f32[4,192,128]{2,1,0:T(8,128)S(1)}, f32[4,192,128]{2,1,0:T(8,128)S(1)}, u32[]{:S(2)}, u32[]{:S(2)}) %collective-permute-start.29) | collective-permute-done | bytes 393248 | tf_op jit(solution)/shard_map/ppermute | solution.py:275
  99.7 5.6 %collective-permute-done.26.outer = f32[4,192,128]{2,1,0:T(8,128)S(1)} collective-permute-done((f32[4,192,128]{2,1,0:T(8,128)S(1)}, f32[4,192,128]{2,1,0:T(8,128)S(1)}, u32[]{:S(2)}, u32[]{:S(2)}) %collective-permute-start.26) | collective-permute-done | bytes 393248 | tf_op jit(solution)/shard_map/ppermute | solution.py:282
  105.6 4.3 %collective-permute-start.34 = (f32[4,192,128]{2,1,0:T(8,128)S(1)}, f32[4,192,128]{2,1,0:T(8,128)S(1)}, u32[]{:S(2)}, u32[]{:S(2)}) collective-permute-start(f32[4,192,128]{2,1,0:T(8,128)S(1)} %shard_map.104.done), channel_id=1, source_target_pairs={{8,16},{9,17},{10,18},{11,19},{12,20},{13,21},{14,22},{15,23},{24,... | collective-permute-start | bytes 1179656 | tf_op jit(solution)/shard_map/ppermute | solution.py:275
  111.0 1.5 %shard_map.106.local = f32[8,192,128]{2,1,0:T(8,128)S(1)} custom-call(f32[40,128]{1,0:T(8,128)S(1)} %get-tuple-element.46.scal, f32[8,192,128]{2,1,0:T(8,128)S(1)} %get-tuple-element.82.cur.prev, f32[8,192,128]{2,1,0:T(8,128)S(1)} %get-tuple-element.78.cur.prev, f32[1536,128]{1,0:T(8,128)S(1)} %bitcast.14, bf16[192,192]{1,0:T(8,128)(2,1)S(1)} %get-tuple-element.48.th, ...), custom_call_target="tpu_custom_call" | custom-call | tf_op jit(solution)/shard_map/pallas_call | solution.py:290
  112.5 6.1 %collective-permute-done.34.outer = f32[4,192,128]{2,1,0:T(8,128)S(1)} collective-permute-done((f32[4,192,128]{2,1,0:T(8,128)S(1)}, f32[4,192,128]{2,1,0:T(8,128)S(1)}, u32[]{:S(2)}, u32[]{:S(2)}) %collective-permute-start.34) | collective-permute-done | bytes 393248 | tf_op jit(solution)/shard_map/ppermute | solution.py:275
  118.7 4.1 %collective-permute-done.31.outer = f32[4,192,128]{2,1,0:T(8,128)S(1)} collective-permute-done((f32[4,192,128]{2,1,0:T(8,128)S(1)}, f32[4,192,128]{2,1,0:T(8,128)S(1)}, u32[]{:S(2)}, u32[]{:S(2)}) %collective-permute-start.31) | collective-permute-done | bytes 393248 | tf_op jit(solution)/shard_map/ppermute | solution.py:282
  123.1 2.2 %collective-permute-start.37 = (f32[4,192,128]{2,1,0:T(8,128)S(1)}, f32[4,192,128]{2,1,0:T(8,128)S(1)}, u32[]{:S(2)}, u32[]{:S(2)}) collective-permute-start(f32[4,192,128]{2,1,0:T(8,128)S(1)} %get-tuple-element.87), channel_id=1, source_target_pairs={{8,16},{9,17},{10,18},{11,19},{12,20},{13,21},{14,22},{15,23},{24,... | collective-permute-start | bytes 1179656 | tf_op jit(solution)/shard_map/ppermute | solution.py:282
  125.3 3.3 %collective-permute-start.36 = (f32[4,192,128]{2,1,0:T(8,128)S(1)}, f32[4,192,128]{2,1,0:T(8,128)S(1)}, u32[]{:S(2)}, u32[]{:S(2)}) collective-permute-start(f32[4,192,128]{2,1,0:T(8,128)S(1)} %shard_map.107.done), channel_id=1, source_target_pairs={{8,16},{9,17},{10,18},{11,19},{12,20},{13,21},{14,22},{15,23},{24,... | collective-permute-start | bytes 1179656 | tf_op jit(solution)/shard_map/ppermute | solution.py:275
  131.1 2.1 %collective-permute-done.38.got_even = f32[192,128]{1,0:T(8,128)S(1)} collective-permute-done((f32[192,128]{1,0:T(8,128)S(1)}, f32[192,128]{1,0:T(8,128)S(1)}, u32[]{:S(2)}, u32[]{:S(2)}) %collective-permute-start.38) | collective-permute-done | bytes 98336 | tf_op jit(solution)/shard_map/ppermute | solution.py:284
  134.0 4.2 %collective-permute-done.36.outer_a = f32[4,192,128]{2,1,0:T(8,128)S(1)} collective-permute-done((f32[4,192,128]{2,1,0:T(8,128)S(1)}, f32[4,192,128]{2,1,0:T(8,128)S(1)}, u32[]{:S(2)}, u32[]{:S(2)}) %collective-permute-start.36) | collective-permute-done | bytes 393248 | tf_op jit(solution)/shard_map/ppermute | solution.py:275
  (87 shorter events, 17.9 us)
Async XLA Ops:
  3.3 13.4 %collective-permute-start = (f32[8,192,128]{2,1,0:T(8,128)S(1)}, f32[8,192,128]{2,1,0:T(8,128)S(1)}, u32[]{:S(2)}, u32[]{:S(2)}) collective-permute-start(f32[8,192,128]{2,1,0:T(8,128)S(1)} %get-tuple-element.47.cur.prev), channel_id=1, source_target_pairs={{0,8},{1,9},{2,10},{3,11},{4,12},{5,13},{6,14},{7,15},{16,24},{17,... | collective-permute-start | bytes 2359304 | tf_op jit(solution)/shard_map/ppermute | solution.py:285
  3.4 13.3 %collective-permute-start.4 = (f32[4,192,128]{2,1,0:T(8,128)S(1)}, f32[4,192,128]{2,1,0:T(8,128)S(1)}, u32[]{:S(2)}, u32[]{:S(2)}) collective-permute-start(f32[4,192,128]{2,1,0:T(8,128)S(1)} %get-tuple-element.61), channel_id=1, source_target_pairs={{8,16},{9,17},{10,18},{11,19},{12,20},{13,21},{14,22},{15,23},{24,... | collective-permute-start | bytes 1179656 | tf_op jit(solution)/shard_map/ppermute | solution.py:275
  9.2 11.8 %collective-permute-start.1 = (f32[4,192,128]{2,1,0:T(8,128)S(1)}, f32[4,192,128]{2,1,0:T(8,128)S(1)}, u32[]{:S(2)}, u32[]{:S(2)}) collective-permute-start(f32[4,192,128]{2,1,0:T(8,128)S(1)} %get-tuple-element.56), channel_id=1, source_target_pairs={{8,16},{9,17},{10,18},{11,19},{12,20},{13,21},{14,22},{15,23},{24,... | collective-permute-start | bytes 1179656 | tf_op jit(solution)/shard_map/ppermute | solution.py:282
  9.2 7.6 %collective-permute-start.2 = (f32[192,128]{1,0:T(8,128)S(1)}, f32[192,128]{1,0:T(8,128)S(1)}, u32[]{:S(2)}, u32[]{:S(2)}) collective-permute-start(f32[192,128]{1,0:T(8,128)S(1)} %get-tuple-element.59), channel_id=1, source_target_pairs={{0,1},{2,3},{4,5},{6,7},{8,9},{10,11},{12,13},{14,15},{16,17},{18,... | collective-permute-start | bytes 294920 | tf_op jit(solution)/shard_map/ppermute | solution.py:284
  10.7 6.2 %collective-permute-start.3 = (f32[192,128]{1,0:T(8,128)S(1)}, f32[192,128]{1,0:T(8,128)S(1)}, u32[]{:S(2)}, u32[]{:S(2)}) collective-permute-start(f32[192,128]{1,0:T(8,128)S(1)} %get-tuple-element.60), channel_id=1, source_target_pairs={{1,2},{3,4},{5,6},{9,10},{11,12},{13,14},{17,18},{19,20},{21,22},{... | collective-permute-start | bytes 294920 | tf_op jit(solution)/shard_map/ppermute | solution.py:283
  21.2 11.8 %collective-permute-start.5 = (f32[8,192,128]{2,1,0:T(8,128)S(1)}, f32[8,192,128]{2,1,0:T(8,128)S(1)}, u32[]{:S(2)}, u32[]{:S(2)}) collective-permute-start(f32[8,192,128]{2,1,0:T(8,128)S(1)} %get-tuple-element.62.cur.prev), channel_id=1, source_target_pairs={{0,8},{1,9},{2,10},{3,11},{4,12},{5,13},{6,14},{7,15},{16,24},{17,... | collective-permute-start | bytes 2359304 | tf_op jit(solution)/shard_map/ppermute | solution.py:285
  21.3 11.7 %collective-permute-start.9 = (f32[4,192,128]{2,1,0:T(8,128)S(1)}, f32[4,192,128]{2,1,0:T(8,128)S(1)}, u32[]{:S(2)}, u32[]{:S(2)}) collective-permute-start(f32[4,192,128]{2,1,0:T(8,128)S(1)} %shard_map.89.done), channel_id=1, source_target_pairs={{8,16},{9,17},{10,18},{11,19},{12,20},{13,21},{14,22},{15,23},{24,... | collective-permute-start | bytes 1179656 | tf_op jit(solution)/shard_map/ppermute | solution.py:275
  26.7 10.8 %collective-permute-start.6 = (f32[4,192,128]{2,1,0:T(8,128)S(1)}, f32[4,192,128]{2,1,0:T(8,128)S(1)}, u32[]{:S(2)}, u32[]{:S(2)}) collective-permute-start(f32[4,192,128]{2,1,0:T(8,128)S(1)} %get-tuple-element.63), channel_id=1, source_target_pairs={{8,16},{9,17},{10,18},{11,19},{12,20},{13,21},{14,22},{15,23},{24,... | collective-permute-start | bytes 1179656 | tf_op jit(solution)/shard_map/ppermute | solution.py:282
  26.8 6.3 %collective-permute-start.7 = (f32[192,128]{1,0:T(8,128)S(1)}, f32[192,128]{1,0:T(8,128)S(1)}, u32[]{:S(2)}, u32[]{:S(2)}) collective-permute-start(f32[192,128]{1,0:T(8,128)S(1)} %get-tuple-element.64), channel_id=1, source_target_pairs={{0,1},{2,3},{4,5},{6,7},{8,9},{10,11},{12,13},{14,15},{16,17},{18,... | collective-permute-start | bytes 294920 | tf_op jit(solution)/shard_map/ppermute | solution.py:284
  27.2 5.9 %collective-permute-start.8 = (f32[192,128]{1,0:T(8,128)S(1)}, f32[192,128]{1,0:T(8,128)S(1)}, u32[]{:S(2)}, u32[]{:S(2)}) collective-permute-start(f32[192,128]{1,0:T(8,128)S(1)} %get-tuple-element.65), channel_id=1, source_target_pairs={{1,2},{3,4},{5,6},{9,10},{11,12},{13,14},{17,18},{19,20},{21,22},{... | collective-permute-start | bytes 294920 | tf_op jit(solution)/shard_map/ppermute | solution.py:283
  37.7 11.0 %collective-permute-start.10 = (f32[8,192,128]{2,1,0:T(8,128)S(1)}, f32[8,192,128]{2,1,0:T(8,128)S(1)}, u32[]{:S(2)}, u32[]{:S(2)}) collective-permute-start(f32[8,192,128]{2,1,0:T(8,128)S(1)} %get-tuple-element.66.cur.prev), channel_id=1, source_target_pairs={{0,8},{1,9},{2,10},{3,11},{4,12},{5,13},{6,14},{7,15},{16,24},{17,... | collective-permute-start | bytes 2359304 | tf_op jit(solution)/shard_map/ppermute | solution.py:285
  37.8 10.9 %collective-permute-start.14 = (f32[4,192,128]{2,1,0:T(8,128)S(1)}, f32[4,192,128]{2,1,0:T(8,128)S(1)}, u32[]{:S(2)}, u32[]{:S(2)}) collective-permute-start(f32[4,192,128]{2,1,0:T(8,128)S(1)} %shard_map.92.done), channel_id=1, source_target_pairs={{8,16},{9,17},{10,18},{11,19},{12,20},{13,21},{14,22},{15,23},{24,... | collective-permute-start | bytes 1179656 | tf_op jit(solution)/shard_map/ppermute | solution.py:275
  43.2 10.8 %collective-permute-start.11 = (f32[4,192,128]{2,1,0:T(8,128)S(1)}, f32[4,192,128]{2,1,0:T(8,128)S(1)}, u32[]{:S(2)}, u32[]{:S(2)}) collective-permute-start(f32[4,192,128]{2,1,0:T(8,128)S(1)} %get-tuple-element.67), channel_id=1, source_target_pairs={{8,16},{9,17},{10,18},{11,19},{12,20},{13,21},{14,22},{15,23},{24,... | collective-permute-start | bytes 1179656 | tf_op jit(solution)/shard_map/ppermute | solution.py:282
  54.2 11.0 %collective-permute-start.15 = (f32[8,192,128]{2,1,0:T(8,128)S(1)}, f32[8,192,128]{2,1,0:T(8,128)S(1)}, u32[]{:S(2)}, u32[]{:S(2)}) collective-permute-start(f32[8,192,128]{2,1,0:T(8,128)S(1)} %get-tuple-element.70.cur.prev), channel_id=1, source_target_pairs={{0,8},{1,9},{2,10},{3,11},{4,12},{5,13},{6,14},{7,15},{16,24},{17,... | collective-permute-start | bytes 2359304 | tf_op jit(solution)/shard_map/ppermute | solution.py:285
  54.3 10.9 %collective-permute-start.19 = (f32[4,192,128]{2,1,0:T(8,128)S(1)}, f32[4,192,128]{2,1,0:T(8,128)S(1)}, u32[]{:S(2)}, u32[]{:S(2)}) collective-permute-start(f32[4,192,128]{2,1,0:T(8,128)S(1)} %shard_map.95.done), channel_id=1, source_target_pairs={{8,16},{9,17},{10,18},{11,19},{12,20},{13,21},{14,22},{15,23},{24,... | collective-permute-start | bytes 1179656 | tf_op jit(solution)/shard_map/ppermute | solution.py:275
  58.6 10.8 %collective-permute-start.16 = (f32[4,192,128]{2,1,0:T(8,128)S(1)}, f32[4,192,128]{2,1,0:T(8,128)S(1)}, u32[]{:S(2)}, u32[]{:S(2)}) collective-permute-start(f32[4,192,128]{2,1,0:T(8,128)S(1)} %get-tuple-element.71), channel_id=1, source_target_pairs={{8,16},{9,17},{10,18},{11,19},{12,20},{13,21},{14,22},{15,23},{24,... | collective-permute-start | bytes 1179656 | tf_op jit(solution)/shard_map/ppermute | solution.py:282
  69.6 11.0 %collective-permute-start.20 = (f32[8,192,128]{2,1,0:T(8,128)S(1)}, f32[8,192,128]{2,1,0:T(8,128)S(1)}, u32[]{:S(2)}, u32[]{:S(2)}) collective-permute-start(f32[8,192,128]{2,1,0:T(8,128)S(1)} %get-tuple-element.74.cur.prev), channel_id=1, source_target_pairs={{0,8},{1,9},{2,10},{3,11},{4,12},{5,13},{6,14},{7,15},{16,24},{17,... | collective-permute-start | bytes 2359304 | tf_op jit(solution)/shard_map/ppermute | solution.py:285
  69.7 10.9 %collective-permute-start.24 = (f32[4,192,128]{2,1,0:T(8,128)S(1)}, f32[4,192,128]{2,1,0:T(8,128)S(1)}, u32[]{:S(2)}, u32[]{:S(2)}) collective-permute-start(f32[4,192,128]{2,1,0:T(8,128)S(1)} %shard_map.98.done), channel_id=1, source_target_pairs={{8,16},{9,17},{10,18},{11,19},{12,20},{13,21},{14,22},{15,23},{24,... | collective-permute-start | bytes 1179656 | tf_op jit(solution)/shard_map/ppermute | solution.py:275
  75.1 12.7 %collective-permute-start.21 = (f32[4,192,128]{2,1,0:T(8,128)S(1)}, f32[4,192,128]{2,1,0:T(8,128)S(1)}, u32[]{:S(2)}, u32[]{:S(2)}) collective-permute-start(f32[4,192,128]{2,1,0:T(8,128)S(1)} %get-tuple-element.75), channel_id=1, source_target_pairs={{8,16},{9,17},{10,18},{11,19},{12,20},{13,21},{14,22},{15,23},{24,... | collective-permute-start | bytes 1179656 | tf_op jit(solution)/shard_map/ppermute | solution.py:282
  87.9 11.6 %collective-permute-start.25 = (f32[8,192,128]{2,1,0:T(8,128)S(1)}, f32[8,192,128]{2,1,0:T(8,128)S(1)}, u32[]{:S(2)}, u32[]{:S(2)}) collective-permute-start(f32[8,192,128]{2,1,0:T(8,128)S(1)} %get-tuple-element.78.cur.prev), channel_id=1, source_target_pairs={{0,8},{1,9},{2,10},{3,11},{4,12},{5,13},{6,14},{7,15},{16,24},{17,... | collective-permute-start | bytes 2359304 | tf_op jit(solution)/shard_map/ppermute | solution.py:285
  88.0 11.5 %collective-permute-start.29 = (f32[4,192,128]{2,1,0:T(8,128)S(1)}, f32[4,192,128]{2,1,0:T(8,128)S(1)}, u32[]{:S(2)}, u32[]{:S(2)}) collective-permute-start(f32[4,192,128]{2,1,0:T(8,128)S(1)} %shard_map.101.done), channel_id=1, source_target_pairs={{8,16},{9,17},{10,18},{11,19},{12,20},{13,21},{14,22},{15,23},{24,... | collective-permute-start | bytes 1179656 | tf_op jit(solution)/shard_map/ppermute | solution.py:275
  92.6 12.7 %collective-permute-start.26 = (f32[4,192,128]{2,1,0:T(8,128)S(1)}, f32[4,192,128]{2,1,0:T(8,128)S(1)}, u32[]{:S(2)}, u32[]{:S(2)}) collective-permute-start(f32[4,192,128]{2,1,0:T(8,128)S(1)} %get-tuple-element.79), channel_id=1, source_target_pairs={{8,16},{9,17},{10,18},{11,19},{12,20},{13,21},{14,22},{15,23},{24,... | collective-permute-start | bytes 1179656 | tf_op jit(solution)/shard_map/ppermute | solution.py:282
  93.5 6.1 %collective-permute-start.27 = (f32[192,128]{1,0:T(8,128)S(1)}, f32[192,128]{1,0:T(8,128)S(1)}, u32[]{:S(2)}, u32[]{:S(2)}) collective-permute-start(f32[192,128]{1,0:T(8,128)S(1)} %get-tuple-element.80), channel_id=1, source_target_pairs={{0,1},{2,3},{4,5},{6,7},{8,9},{10,11},{12,13},{14,15},{16,17},{18,... | collective-permute-start | bytes 294920 | tf_op jit(solution)/shard_map/ppermute | solution.py:284
  93.5 6.1 %collective-permute-start.28 = (f32[192,128]{1,0:T(8,128)S(1)}, f32[192,128]{1,0:T(8,128)S(1)}, u32[]{:S(2)}, u32[]{:S(2)}) collective-permute-start(f32[192,128]{1,0:T(8,128)S(1)} %get-tuple-element.81), channel_id=1, source_target_pairs={{1,2},{3,4},{5,6},{9,10},{11,12},{13,14},{17,18},{19,20},{21,22},{... | collective-permute-start | bytes 294920 | tf_op jit(solution)/shard_map/ppermute | solution.py:283
  105.5 13.1 %collective-permute-start.30 = (f32[8,192,128]{2,1,0:T(8,128)S(1)}, f32[8,192,128]{2,1,0:T(8,128)S(1)}, u32[]{:S(2)}, u32[]{:S(2)}) collective-permute-start(f32[8,192,128]{2,1,0:T(8,128)S(1)} %get-tuple-element.82.cur.prev), channel_id=1, source_target_pairs={{0,8},{1,9},{2,10},{3,11},{4,12},{5,13},{6,14},{7,15},{16,24},{17,... | collective-permute-start | bytes 2359304 | tf_op jit(solution)/shard_map/ppermute | solution.py:285
  105.6 13.0 %collective-permute-start.34 = (f32[4,192,128]{2,1,0:T(8,128)S(1)}, f32[4,192,128]{2,1,0:T(8,128)S(1)}, u32[]{:S(2)}, u32[]{:S(2)}) collective-permute-start(f32[4,192,128]{2,1,0:T(8,128)S(1)} %shard_map.104.done), channel_id=1, source_target_pairs={{8,16},{9,17},{10,18},{11,19},{12,20},{13,21},{14,22},{15,23},{24,... | collective-permute-start | bytes 1179656 | tf_op jit(solution)/shard_map/ppermute | solution.py:275
  109.9 12.9 %collective-permute-start.31 = (f32[4,192,128]{2,1,0:T(8,128)S(1)}, f32[4,192,128]{2,1,0:T(8,128)S(1)}, u32[]{:S(2)}, u32[]{:S(2)}) collective-permute-start(f32[4,192,128]{2,1,0:T(8,128)S(1)} %get-tuple-element.83), channel_id=1, source_target_pairs={{8,16},{9,17},{10,18},{11,19},{12,20},{13,21},{14,22},{15,23},{24,... | collective-permute-start | bytes 1179656 | tf_op jit(solution)/shard_map/ppermute | solution.py:282
  111.0 7.7 %collective-permute-start.32 = (f32[192,128]{1,0:T(8,128)S(1)}, f32[192,128]{1,0:T(8,128)S(1)}, u32[]{:S(2)}, u32[]{:S(2)}) collective-permute-start(f32[192,128]{1,0:T(8,128)S(1)} %get-tuple-element.84), channel_id=1, source_target_pairs={{0,1},{2,3},{4,5},{6,7},{8,9},{10,11},{12,13},{14,15},{16,17},{18,... | collective-permute-start | bytes 294920 | tf_op jit(solution)/shard_map/ppermute | solution.py:284
  111.0 7.7 %collective-permute-start.33 = (f32[192,128]{1,0:T(8,128)S(1)}, f32[192,128]{1,0:T(8,128)S(1)}, u32[]{:S(2)}, u32[]{:S(2)}) collective-permute-start(f32[192,128]{1,0:T(8,128)S(1)} %get-tuple-element.85), channel_id=1, source_target_pairs={{1,2},{3,4},{5,6},{9,10},{11,12},{13,14},{17,18},{19,20},{21,22},{... | collective-permute-start | bytes 294920 | tf_op jit(solution)/shard_map/ppermute | solution.py:283
  123.0 15.2 %collective-permute-start.35 = (f32[8,192,128]{2,1,0:T(8,128)S(1)}, f32[8,192,128]{2,1,0:T(8,128)S(1)}, u32[]{:S(2)}, u32[]{:S(2)}) collective-permute-start(f32[8,192,128]{2,1,0:T(8,128)S(1)} %get-tuple-element.86.wave.cur), channel_id=1, source_target_pairs={{0,8},{1,9},{2,10},{3,11},{4,12},{5,13},{6,14},{7,15},{16,24},{17,... | collective-permute-start | bytes 2359304 | tf_op jit(solution)/shard_map/ppermute | solution.py:285
  123.1 10.9 %collective-permute-start.37 = (f32[4,192,128]{2,1,0:T(8,128)S(1)}, f32[4,192,128]{2,1,0:T(8,128)S(1)}, u32[]{:S(2)}, u32[]{:S(2)}) collective-permute-start(f32[4,192,128]{2,1,0:T(8,128)S(1)} %get-tuple-element.87), channel_id=1, source_target_pairs={{8,16},{9,17},{10,18},{11,19},{12,20},{13,21},{14,22},{15,23},{24,... | collective-permute-start | bytes 1179656 | tf_op jit(solution)/shard_map/ppermute | solution.py:282
  125.3 12.9 %collective-permute-start.36 = (f32[4,192,128]{2,1,0:T(8,128)S(1)}, f32[4,192,128]{2,1,0:T(8,128)S(1)}, u32[]{:S(2)}, u32[]{:S(2)}) collective-permute-start(f32[4,192,128]{2,1,0:T(8,128)S(1)} %shard_map.107.done), channel_id=1, source_target_pairs={{8,16},{9,17},{10,18},{11,19},{12,20},{13,21},{14,22},{15,23},{24,... | collective-permute-start | bytes 1179656 | tf_op jit(solution)/shard_map/ppermute | solution.py:275
  (14 other events, 60.5 us)
where the time goes:
time: 140 us; the launch traced here: 139 us
  waiting for transfers between devices  69.3 us (50%)
  starting transfers between devices  46.7 us (33%)
  Pallas kernels  17.7 us (13%)
  local copies, waits for them, and re-layouts  3.85 us (3%)
  between operations  1.69 us (1%)
    ppermute x8, starting transfers between devices, on_device(): new_outer_a = lax.ppermute(a, axes, k_odd)  38.3 us
    ppermute x8, waiting for transfers between devices, on_device(): outer_b = lax.ppermute(b, axes, k_odd)  35.2 us
    ppermute x8, waiting for transfers between devices, on_device(): new_outer_a = lax.ppermute(a, axes, k_odd)  32 us
    pallas_call x8, Pallas kernels, on_device(): local_call[n == 0]  11.8 us
    ppermute x8, starting transfers between devices, on_device(): outer_b = lax.ppermute(b, axes, k_odd)  5.7 us
    unnamed x12, local copies, waits for them, and re-layouts  3.85 us
  transfers between devices with their start and end apart: 40, of which 17 were waited for; matrix products, arithmetic and copies ran while one was open for 0% of the time, Pallas kernels for 10%

commit v1 on v0

--- a/solution.py
+++ b/solution.py
@@ -48,7 +48,7 @@
 def groups(rows):
     quarter = rows // 4
     inside = list(range(quarter, rows - quarter))
-    return inside, [n for n in range(rows) if n not in inside]
+    return [n for n in range(rows) if n not in inside], inside
 
 
 def fade_row(rows, n):
@@ -133,21 +133,28 @@
     )
 
 
-def start_kernel(rows, where, wave, first_group, second_group, whole, send_even, send_odd):
+def begin_kernel(rows, where, wave, out, send_even, send_odd):
     nrot, width = send_even.shape
-    inside, outside = groups(rows)
-    alive = lax.broadcasted_iota(jnp.int32, (nrot, width), 0) >= where[2]
-    for n in range(rows):
-        v = jnp.where(alive, wave[strided(rows, n, nrot), :], 0.0)
-        whole[n] = v
-        if n in inside:
-            first_group[inside.index(n)] = v
-        else:
-            second_group[outside.index(n)] = v
-    odd = where[1] % 2 == 1
-    low, high = whole[0], whole[rows - 1]
+    outside, _ = groups(rows)
+    alive = lax.broadcasted_iota(jnp.int32, (nrot, width), 0) >= where[2:3, :]
+    for i, n in enumerate(outside):
+        out[i] = jnp.where(alive, wave[strided(rows, n, nrot), :], 0.0)
+    odd = (where[1:2, :] & 1) == 1
+    low, high = out[0], out[len(outside) - 1]
     send_even[...] = jnp.where(odd, low, high)
     send_odd[...] = jnp.where(odd, high, low)
+
+
+def rest_kernel(rows, where, wave, done, out, whole):
+    nrot, width = out.shape[1:]
+    outside, inside = groups(rows)
+    alive = lax.broadcasted_iota(jnp.int32, (nrot, width), 0) >= where[2:3, :]
+    for i, n in enumerate(inside):
+        v = jnp.where(alive, wave[strided(rows, n, nrot), :], 0.0)
+        out[i] = v
+        whole[n] = v
+    for i, n in enumerate(outside):
+        whole[n] = done[i]
 
 
 def local_kernel(rows, opening, scal, cur, prev, pot, th, tl, bh, bl, kin2, rotq, qp, live, out):
@@ -155,10 +162,12 @@
     for i in range(0, rows, 2):
         x = [cur[i], cur[i + 1]]
         xh, xl = split(jnp.concatenate(x, axis=1))
-        angular = mul(th[...], xh) + mul(tl[...], xh) + mul(th[...], xl)
+        two = mul(jnp.concatenate([th[...], tl[...]], axis=0), xh)
+        angular = two[:nrot] + two[nrot:] + mul(th[...], xl)
         y = jnp.concatenate([pot[strided(rows, i + h, nrot), :] for h in range(2)], axis=1) * angular
         yh, yl = split(y)
-        back = mul(bh[...], yh) + mul(bl[...], yh) + mul(bh[...], yl)
+        two = mul(jnp.concatenate([bh[...], bl[...]], axis=0), yh)
+        back = two[:nrot] + two[nrot:] + mul(bh[...], yl)
         for h in range(2):
             n = i + h
             part = slice(h * width, (h + 1) * width)
@@ -186,24 +195,24 @@
     return new
 
 
-def inside_kernel(rows, scal, local, inner, outer, s_in, s_out, out):
-    inside, _ = groups(rows)
-    for i, n in enumerate(inside):
-        out[i] = plane(rows, n, scal, local, inner, outer[i], s_in, s_out, None)
-
-
-def outside_kernel(rows, scal, local, inner, outer, s_in, s_out, got_even, got_odd, done, *outs):
-    out, whole, send_even, send_odd = outs
-    inside, outside = groups(rows)
+def outside_kernel(rows, scal, local, inner, outer, s_in, s_out, got_even, got_odd, *outs):
+    out, send_even, send_odd = outs
+    outside, _ = groups(rows)
     for i, n in enumerate(outside):
-        v = plane(rows, n, scal, local, inner, outer[i], s_in, s_out, (got_even, got_odd))
-        out[i] = v
-        whole[n] = v
-    low, high = whole[0], whole[rows - 1]
+        out[i] = plane(rows, n, scal, local, inner, outer[i], s_in, s_out, (got_even, got_odd))
+    low, high = out[0], out[len(outside) - 1]
     odd = at_row(scal, halo_row(rows, 4)) > 0.5
     send_even[...] = jnp.where(odd, low, high)
     send_odd[...] = jnp.where(odd, high, low)
+
+
+def inside_kernel(rows, scal, local, inner, outer, s_in, s_out, done, out, whole):
+    outside, inside = groups(rows)
     for i, n in enumerate(inside):
+        v = plane(rows, n, scal, local, inner, outer[i], s_in, s_out, None)
+        out[i] = v
+        whole[n] = v
+    for i, n in enumerate(outside):
         whole[n] = done[i]
 
 
@@ -231,8 +240,8 @@
     f32 = lambda *shape: jax.ShapeDtypeStruct(shape, jnp.float32)
     b16 = lambda *shape: jax.ShapeDtypeStruct(shape, jnp.bfloat16)
     face, block = f32(nrot, width), f32(rows, nrot, width)
-    inside, outside = groups(rows)
-    part_a, part_b = f32(len(inside), nrot, width), f32(len(outside), nrot, width)
+    outside, inside = groups(rows)
+    part_a, part_b = f32(len(outside), nrot, width), f32(len(inside), nrot, width)
 
     def call(kernel, ins, outs, *static):
         return pl.pallas_call(
@@ -258,27 +267,31 @@
         nka,
         nrad,
     )
-    start = call(start_kernel, [SMEM, VMEM], [part_a, part_b, block, face, face])
+    begin = call(begin_kernel, [VMEM] * 2, [part_a, face, face])
+    rest = call(rest_kernel, [VMEM] * 3, [part_b, block])
     local_call = [call(local_kernel, [VMEM] * 12, block, o) for o in (False, True)]
-    inside_call = call(inside_kernel, [VMEM] * 6, part_a)
-    outside_call = call(outside_kernel, [VMEM] * 9, [part_b, block, face, face])
+    outside_call = call(outside_kernel, [VMEM] * 8, [part_a, face, face])
+    inside_call = call(inside_kernel, [VMEM] * 7, [part_b, block])
     finish = call(finish_kernel, [VMEM] * 9, f32(*flat))
     turn_back = call(turn_kernel, [VMEM], f32(*flat))
 
-    a, b, whole, send_even, send_odd = start(where, cur_wave.reshape(flat))
+    opening = cur_wave.reshape(flat)
+    lanes = jnp.broadcast_to(where[:, None], (3, width))
+    a, send_even, send_odd = begin(lanes, opening)
     prev = prev_wave.reshape(flat)
     pot = potential.reshape(flat)
     total = KICKS * STEPS
     for n in range(total):
         if n:
-            a = inside_call(scal, local, inner, outer_a, s_in, s_out)
-        new_outer_a = lax.ppermute(a, axes, k_odd)
-        if n:
-            b, made, send_even, send_odd = outside_call(
-                scal, local, inner, outer_b, s_in, s_out, got_even, got_odd, a
-            )
+            a, send_even, send_odd = outside_call(
+                scal, local, inner, outer_a, s_in, s_out, got_even, got_odd
+            )
+        outer_a = lax.ppermute(a, axes, k_odd)
+        if n == 0:
+            b, whole = rest(lanes, opening, a)
+        else:
+            b, made = inside_call(scal, local, inner, outer_b, s_in, s_out, a)
             prev, whole = whole, made
-        outer_a = new_outer_a
         outer_b = lax.ppermute(b, axes, k_odd)
         got_odd = lax.ppermute(send_odd, axes, r_odd)
         got_even = lax.ppermute(send_even, axes, r_even)

time: 140 us -> 139 us (level)
  the two profiles are of different devices: /device:TPU:16 before, /device:TPU:30 now
where the time goes in v1:
time: 139 us
  waiting for transfers between devices  71.5 us (51%)
  starting transfers between devices  47 us (34%)
  Pallas kernels  16.7 us (12%)
  local copies, waits for them, and re-layouts  1.87 us (1%)
  between operations  1.54 us (1%)
    ppermute x8, starting transfers between devices, on_device(): outer_a = lax.ppermute(a, axes, k_odd)  38.6 us
    ppermute x8, waiting for transfers between devices, on_device(): outer_b = lax.ppermute(b, axes, k_odd)  35.4 us
    ppermute x8, waiting for transfers between devices, on_device(): got_even = lax.ppermute(send_even, axes, r_even)  22.3 us
    ppermute x8, waiting for transfers between devices, on_device(): outer_a = lax.ppermute(a, axes, k_odd)  13.8 us
    pallas_call x8, Pallas kernels, on_device(): local_call[n == 0]  11.2 us
    ppermute x8, starting transfers between devices, on_device(): outer_b = lax.ppermute(b, axes, k_odd)  6.86 us
  transfers between devices with their start and end apart: 40, of which 24 were waited for; matrix products, arithmetic and copies ran while one was open for 0% of the time, Pallas kernels for 10%

profile of v1, /device:TPU:30, one launch (start us, length us, event | category | flops | bytes accessed | tf_op | source)
XLA Modules:
  0.0 138.7 jit_solution(14074451792982985337)
XLA Ops:
  2.9 6.6 %collective-permute-start.2 = (f32[4,192,128]{2,1,0:T(8,128)S(1)}, f32[4,192,128]{2,1,0:T(8,128)S(1)}, u32[]{:S(2)}, u32[]{:S(2)}) collective-permute-start(f32[4,192,128]{2,1,0:T(8,128)S(1)} %get-tuple-element.54.done), channel_id=1, source_target_pairs={{8,16},{9,17},{10,18},{11,19},{12,20},{13,21},{14,22},{15,23},{24,... | collective-permute-start | bytes 1179656 | tf_op jit(solution)/shard_map/ppermute | solution.py:289
  11.9 1.5 %shard_map.89.local = f32[8,192,128]{2,1,0:T(8,128)S(1)} custom-call(f32[40,128]{1,0:T(8,128)S(1)} %get-tuple-element.53.scal, f32[8,192,128]{2,1,0:T(8,128)S(1)} %get-tuple-element.55.cur.prev, f32[1536,128]{1,0:T(8,128)S(1)} %bitcast.18, f32[1536,128]{1,0:T(8,128)S(1)} %bitcast.8, bf16[192,192]{1,0:T(8,128)(2,1)S(1)} %get-tuple-element.56.th, ...), custom_call_target="tpu_custom_call" | custom-call | tf_op jit(solution)/shard_map/pallas_call | solution.py:303
  14.2 2.2 %collective-permute-done.2.outer = f32[4,192,128]{2,1,0:T(8,128)S(1)} collective-permute-done((f32[4,192,128]{2,1,0:T(8,128)S(1)}, f32[4,192,128]{2,1,0:T(8,128)S(1)}, u32[]{:S(2)}, u32[]{:S(2)}) %collective-permute-start.2) | collective-permute-done | bytes 393248 | tf_op jit(solution)/shard_map/ppermute | solution.py:289
  16.6 4.5 %collective-permute-done.1.outer = f32[4,192,128]{2,1,0:T(8,128)S(1)} collective-permute-done((f32[4,192,128]{2,1,0:T(8,128)S(1)}, f32[4,192,128]{2,1,0:T(8,128)S(1)}, u32[]{:S(2)}, u32[]{:S(2)}) %collective-permute-start.1) | collective-permute-done | bytes 393248 | tf_op jit(solution)/shard_map/ppermute | solution.py:295
  21.4 5.7 %collective-permute-start.7 = (f32[4,192,128]{2,1,0:T(8,128)S(1)}, f32[4,192,128]{2,1,0:T(8,128)S(1)}, u32[]{:S(2)}, u32[]{:S(2)}) collective-permute-start(f32[4,192,128]{2,1,0:T(8,128)S(1)} %get-tuple-element.69.done), channel_id=1, source_target_pairs={{8,16},{9,17},{10,18},{11,19},{12,20},{13,21},{14,22},{15,23},{24,... | collective-permute-start | bytes 1179656 | tf_op jit(solution)/shard_map/ppermute | solution.py:289
  27.1 1.4 shard_map.92.local
  28.5 3.2 %collective-permute-done.8.got_even = f32[192,128]{1,0:T(8,128)S(1)} collective-permute-done((f32[192,128]{1,0:T(8,128)S(1)}, f32[192,128]{1,0:T(8,128)S(1)}, u32[]{:S(2)}, u32[]{:S(2)}) %collective-permute-start.8) | collective-permute-done | bytes 98336 | tf_op jit(solution)/shard_map/ppermute | solution.py:297
  32.7 5.2 %collective-permute-done.6.outer = f32[4,192,128]{2,1,0:T(8,128)S(1)} collective-permute-done((f32[4,192,128]{2,1,0:T(8,128)S(1)}, f32[4,192,128]{2,1,0:T(8,128)S(1)}, u32[]{:S(2)}, u32[]{:S(2)}) %collective-permute-start.6) | collective-permute-done | bytes 393248 | tf_op jit(solution)/shard_map/ppermute | solution.py:295
  38.1 4.3 %collective-permute-start.12 = (f32[4,192,128]{2,1,0:T(8,128)S(1)}, f32[4,192,128]{2,1,0:T(8,128)S(1)}, u32[]{:S(2)}, u32[]{:S(2)}) collective-permute-start(f32[4,192,128]{2,1,0:T(8,128)S(1)} %get-tuple-element.74.done), channel_id=1, source_target_pairs={{8,16},{9,17},{10,18},{11,19},{12,20},{13,21},{14,22},{15,23},{24,... | collective-permute-start | bytes 1179656 | tf_op jit(solution)/shard_map/ppermute | solution.py:289
  44.9 3.2 %collective-permute-done.13.got_even = f32[192,128]{1,0:T(8,128)S(1)} collective-permute-done((f32[192,128]{1,0:T(8,128)S(1)}, f32[192,128]{1,0:T(8,128)S(1)}, u32[]{:S(2)}, u32[]{:S(2)}) %collective-permute-start.13) | collective-permute-done | bytes 98336 | tf_op jit(solution)/shard_map/ppermute | solution.py:297
  49.2 4.0 %collective-permute-done.11.outer = f32[4,192,128]{2,1,0:T(8,128)S(1)} collective-permute-done((f32[4,192,128]{2,1,0:T(8,128)S(1)}, f32[4,192,128]{2,1,0:T(8,128)S(1)}, u32[]{:S(2)}, u32[]{:S(2)}) %collective-permute-start.11) | collective-permute-done | bytes 393248 | tf_op jit(solution)/shard_map/ppermute | solution.py:295
  53.4 4.3 %collective-permute-start.17 = (f32[4,192,128]{2,1,0:T(8,128)S(1)}, f32[4,192,128]{2,1,0:T(8,128)S(1)}, u32[]{:S(2)}, u32[]{:S(2)}) collective-permute-start(f32[4,192,128]{2,1,0:T(8,128)S(1)} %get-tuple-element.79.done), channel_id=1, source_target_pairs={{8,16},{9,17},{10,18},{11,19},{12,20},{13,21},{14,22},{15,23},{24,... | collective-permute-start | bytes 1179656 | tf_op jit(solution)/shard_map/ppermute | solution.py:289
  58.9 1.4 shard_map.98.local
  60.3 3.2 %collective-permute-done.18.got_even = f32[192,128]{1,0:T(8,128)S(1)} collective-permute-done((f32[192,128]{1,0:T(8,128)S(1)}, f32[192,128]{1,0:T(8,128)S(1)}, u32[]{:S(2)}, u32[]{:S(2)}) %collective-permute-start.18) | collective-permute-done | bytes 98336 | tf_op jit(solution)/shard_map/ppermute | solution.py:297
  64.5 4.0 %collective-permute-done.16.outer = f32[4,192,128]{2,1,0:T(8,128)S(1)} collective-permute-done((f32[4,192,128]{2,1,0:T(8,128)S(1)}, f32[4,192,128]{2,1,0:T(8,128)S(1)}, u32[]{:S(2)}, u32[]{:S(2)}) %collective-permute-start.16) | collective-permute-done | bytes 393248 | tf_op jit(solution)/shard_map/ppermute | solution.py:295
  68.8 5.7 %collective-permute-start.22 = (f32[4,192,128]{2,1,0:T(8,128)S(1)}, f32[4,192,128]{2,1,0:T(8,128)S(1)}, u32[]{:S(2)}, u32[]{:S(2)}) collective-permute-start(f32[4,192,128]{2,1,0:T(8,128)S(1)} %get-tuple-element.84.done), channel_id=1, source_target_pairs={{8,16},{9,17},{10,18},{11,19},{12,20},{13,21},{14,22},{15,23},{24,... | collective-permute-start | bytes 1179656 | tf_op jit(solution)/shard_map/ppermute | solution.py:289
  75.9 3.2 %collective-permute-done.23.got_even = f32[192,128]{1,0:T(8,128)S(1)} collective-permute-done((f32[192,128]{1,0:T(8,128)S(1)}, f32[192,128]{1,0:T(8,128)S(1)}, u32[]{:S(2)}, u32[]{:S(2)}) %collective-permute-start.23) | collective-permute-done | bytes 98336 | tf_op jit(solution)/shard_map/ppermute | solution.py:297
  80.1 7.1 %collective-permute-done.21.outer = f32[4,192,128]{2,1,0:T(8,128)S(1)} collective-permute-done((f32[4,192,128]{2,1,0:T(8,128)S(1)}, f32[4,192,128]{2,1,0:T(8,128)S(1)}, u32[]{:S(2)}, u32[]{:S(2)}) %collective-permute-start.21) | collective-permute-done | bytes 393248 | tf_op jit(solution)/shard_map/ppermute | solution.py:295
  87.5 4.5 %collective-permute-start.27 = (f32[4,192,128]{2,1,0:T(8,128)S(1)}, f32[4,192,128]{2,1,0:T(8,128)S(1)}, u32[]{:S(2)}, u32[]{:S(2)}) collective-permute-start(f32[4,192,128]{2,1,0:T(8,128)S(1)} %get-tuple-element.89.done), channel_id=1, source_target_pairs={{8,16},{9,17},{10,18},{11,19},{12,20},{13,21},{14,22},{15,23},{24,... | collective-permute-start | bytes 1179656 | tf_op jit(solution)/shard_map/ppermute | solution.py:289
  92.9 1.4 %shard_map.104.local = f32[8,192,128]{2,1,0:T(8,128)S(1)} custom-call(f32[40,128]{1,0:T(8,128)S(1)} %get-tuple-element.53.scal, f32[8,192,128]{2,1,0:T(8,128)S(1)} %get-tuple-element.90.cur.prev, f32[8,192,128]{2,1,0:T(8,128)S(1)} %get-tuple-element.85.cur.prev, f32[1536,128]{1,0:T(8,128)S(1)} %bitcast.13, bf16[192,192]{1,0:T(8,128)(2,1)S(1)} %get-tuple-element.56.th, ...), custom_call_target="tpu_custom_call" | custom-call | tf_op jit(solution)/shard_map/pallas_call | solution.py:303
  94.3 3.2 %collective-permute-done.28.got_even = f32[192,128]{1,0:T(8,128)S(1)} collective-permute-done((f32[192,128]{1,0:T(8,128)S(1)}, f32[192,128]{1,0:T(8,128)S(1)}, u32[]{:S(2)}, u32[]{:S(2)}) %collective-permute-start.28) | collective-permute-done | bytes 98336 | tf_op jit(solution)/shard_map/ppermute | solution.py:297
  99.0 5.7 %collective-permute-done.26.outer = f32[4,192,128]{2,1,0:T(8,128)S(1)} collective-permute-done((f32[4,192,128]{2,1,0:T(8,128)S(1)}, f32[4,192,128]{2,1,0:T(8,128)S(1)}, u32[]{:S(2)}, u32[]{:S(2)}) %collective-permute-start.26) | collective-permute-done | bytes 393248 | tf_op jit(solution)/shard_map/ppermute | solution.py:295
  104.9 3.9 %collective-permute-start.32 = (f32[4,192,128]{2,1,0:T(8,128)S(1)}, f32[4,192,128]{2,1,0:T(8,128)S(1)}, u32[]{:S(2)}, u32[]{:S(2)}) collective-permute-start(f32[4,192,128]{2,1,0:T(8,128)S(1)} %get-tuple-element.94.done), channel_id=1, source_target_pairs={{8,16},{9,17},{10,18},{11,19},{12,20},{13,21},{14,22},{15,23},{24,... | collective-permute-start | bytes 1179656 | tf_op jit(solution)/shard_map/ppermute | solution.py:289
  108.9 1.5 %collective-permute-start.31 = (f32[4,192,128]{2,1,0:T(8,128)S(1)}, f32[4,192,128]{2,1,0:T(8,128)S(1)}, u32[]{:S(2)}, u32[]{:S(2)}) collective-permute-start(f32[4,192,128]{2,1,0:T(8,128)S(1)} %get-tuple-element.96), channel_id=1, source_target_pairs={{8,16},{9,17},{10,18},{11,19},{12,20},{13,21},{14,22},{15,23},{24,... | collective-permute-start | bytes 1179656 | tf_op jit(solution)/shard_map/ppermute | solution.py:295
  111.8 3.2 %collective-permute-done.33.got_even = f32[192,128]{1,0:T(8,128)S(1)} collective-permute-done((f32[192,128]{1,0:T(8,128)S(1)}, f32[192,128]{1,0:T(8,128)S(1)}, u32[]{:S(2)}, u32[]{:S(2)}) %collective-permute-start.33) | collective-permute-done | bytes 98336 | tf_op jit(solution)/shard_map/ppermute | solution.py:297
  115.0 2.9 %collective-permute-done.32.outer = f32[4,192,128]{2,1,0:T(8,128)S(1)} collective-permute-done((f32[4,192,128]{2,1,0:T(8,128)S(1)}, f32[4,192,128]{2,1,0:T(8,128)S(1)}, u32[]{:S(2)}, u32[]{:S(2)}) %collective-permute-start.32) | collective-permute-done | bytes 393248 | tf_op jit(solution)/shard_map/ppermute | solution.py:289
  118.1 4.0 %collective-permute-done.31.outer = f32[4,192,128]{2,1,0:T(8,128)S(1)} collective-permute-done((f32[4,192,128]{2,1,0:T(8,128)S(1)}, f32[4,192,128]{2,1,0:T(8,128)S(1)}, u32[]{:S(2)}, u32[]{:S(2)}) %collective-permute-start.31) | collective-permute-done | bytes 393248 | tf_op jit(solution)/shard_map/ppermute | solution.py:295
  122.4 1.8 %collective-permute-start.37 = (f32[4,192,128]{2,1,0:T(8,128)S(1)}, f32[4,192,128]{2,1,0:T(8,128)S(1)}, u32[]{:S(2)}, u32[]{:S(2)}) collective-permute-start(f32[4,192,128]{2,1,0:T(8,128)S(1)} %get-tuple-element.101), channel_id=1, source_target_pairs={{8,16},{9,17},{10,18},{11,19},{12,20},{13,21},{14,22},{15,23},{24,... | collective-permute-start | bytes 1179656 | tf_op jit(solution)/shard_map/ppermute | solution.py:295
  124.2 3.6 %collective-permute-start.36 = (f32[4,192,128]{2,1,0:T(8,128)S(1)}, f32[4,192,128]{2,1,0:T(8,128)S(1)}, u32[]{:S(2)}, u32[]{:S(2)}) collective-permute-start(f32[4,192,128]{2,1,0:T(8,128)S(1)} %get-tuple-element.99.done), channel_id=1, source_target_pairs={{8,16},{9,17},{10,18},{11,19},{12,20},{13,21},{14,22},{15,23},{24,... | collective-permute-start | bytes 1179656 | tf_op jit(solution)/shard_map/ppermute | solution.py:289
  127.9 1.4 shard_map.111.local
  130.3 2.1 %collective-permute-done.38.got_even = f32[192,128]{1,0:T(8,128)S(1)} collective-permute-done((f32[192,128]{1,0:T(8,128)S(1)}, f32[192,128]{1,0:T(8,128)S(1)}, u32[]{:S(2)}, u32[]{:S(2)}) %collective-permute-start.38) | collective-permute-done | bytes 98336 | tf_op jit(solution)/shard_map/ppermute | solution.py:297
  133.3 4.2 %collective-permute-done.36.outer_a = f32[4,192,128]{2,1,0:T(8,128)S(1)} collective-permute-done((f32[4,192,128]{2,1,0:T(8,128)S(1)}, f32[4,192,128]{2,1,0:T(8,128)S(1)}, u32[]{:S(2)}, u32[]{:S(2)}) %collective-permute-start.36) | collective-permute-done | bytes 393248 | tf_op jit(solution)/shard_map/ppermute | solution.py:289
  (89 shorter events, 22.8 us)
Async XLA Ops:
  2.8 13.6 %collective-permute-start = (f32[8,192,128]{2,1,0:T(8,128)S(1)}, f32[8,192,128]{2,1,0:T(8,128)S(1)}, u32[]{:S(2)}, u32[]{:S(2)}) collective-permute-start(f32[8,192,128]{2,1,0:T(8,128)S(1)} %get-tuple-element.55.cur.prev), channel_id=1, source_target_pairs={{0,8},{1,9},{2,10},{3,11},{4,12},{5,13},{6,14},{7,15},{16,24},{17,... | collective-permute-start | bytes 2359304 | tf_op jit(solution)/shard_map/ppermute | solution.py:298
  2.9 13.5 %collective-permute-start.2 = (f32[4,192,128]{2,1,0:T(8,128)S(1)}, f32[4,192,128]{2,1,0:T(8,128)S(1)}, u32[]{:S(2)}, u32[]{:S(2)}) collective-permute-start(f32[4,192,128]{2,1,0:T(8,128)S(1)} %get-tuple-element.54.done), channel_id=1, source_target_pairs={{8,16},{9,17},{10,18},{11,19},{12,20},{13,21},{14,22},{15,23},{24,... | collective-permute-start | bytes 1179656 | tf_op jit(solution)/shard_map/ppermute | solution.py:289
  9.6 11.6 %collective-permute-start.1 = (f32[4,192,128]{2,1,0:T(8,128)S(1)}, f32[4,192,128]{2,1,0:T(8,128)S(1)}, u32[]{:S(2)}, u32[]{:S(2)}) collective-permute-start(f32[4,192,128]{2,1,0:T(8,128)S(1)} %get-tuple-element.64), channel_id=1, source_target_pairs={{8,16},{9,17},{10,18},{11,19},{12,20},{13,21},{14,22},{15,23},{24,... | collective-permute-start | bytes 1179656 | tf_op jit(solution)/shard_map/ppermute | solution.py:295
  9.6 4.6 %collective-permute-start.3 = (f32[192,128]{1,0:T(8,128)S(1)}, f32[192,128]{1,0:T(8,128)S(1)}, u32[]{:S(2)}, u32[]{:S(2)}) collective-permute-start(f32[192,128]{1,0:T(8,128)S(1)} %get-tuple-element.67), channel_id=1, source_target_pairs={{0,1},{2,3},{4,5},{6,7},{8,9},{10,11},{12,13},{14,15},{16,17},{18,... | collective-permute-start | bytes 294920 | tf_op jit(solution)/shard_map/ppermute | solution.py:297
  21.3 11.2 %collective-permute-start.5 = (f32[8,192,128]{2,1,0:T(8,128)S(1)}, f32[8,192,128]{2,1,0:T(8,128)S(1)}, u32[]{:S(2)}, u32[]{:S(2)}) collective-permute-start(f32[8,192,128]{2,1,0:T(8,128)S(1)} %get-tuple-element.70.cur.prev), channel_id=1, source_target_pairs={{0,8},{1,9},{2,10},{3,11},{4,12},{5,13},{6,14},{7,15},{16,24},{17,... | collective-permute-start | bytes 2359304 | tf_op jit(solution)/shard_map/ppermute | solution.py:298
  21.4 11.1 %collective-permute-start.7 = (f32[4,192,128]{2,1,0:T(8,128)S(1)}, f32[4,192,128]{2,1,0:T(8,128)S(1)}, u32[]{:S(2)}, u32[]{:S(2)}) collective-permute-start(f32[4,192,128]{2,1,0:T(8,128)S(1)} %get-tuple-element.69.done), channel_id=1, source_target_pairs={{8,16},{9,17},{10,18},{11,19},{12,20},{13,21},{14,22},{15,23},{24,... | collective-permute-start | bytes 1179656 | tf_op jit(solution)/shard_map/ppermute | solution.py:289
  27.0 10.8 %collective-permute-start.6 = (f32[4,192,128]{2,1,0:T(8,128)S(1)}, f32[4,192,128]{2,1,0:T(8,128)S(1)}, u32[]{:S(2)}, u32[]{:S(2)}) collective-permute-start(f32[4,192,128]{2,1,0:T(8,128)S(1)} %get-tuple-element.71), channel_id=1, source_target_pairs={{8,16},{9,17},{10,18},{11,19},{12,20},{13,21},{14,22},{15,23},{24,... | collective-permute-start | bytes 1179656 | tf_op jit(solution)/shard_map/ppermute | solution.py:295
  27.1 4.6 %collective-permute-start.8 = (f32[192,128]{1,0:T(8,128)S(1)}, f32[192,128]{1,0:T(8,128)S(1)}, u32[]{:S(2)}, u32[]{:S(2)}) collective-permute-start(f32[192,128]{1,0:T(8,128)S(1)} %get-tuple-element.72), channel_id=1, source_target_pairs={{0,1},{2,3},{4,5},{6,7},{8,9},{10,11},{12,13},{14,15},{16,17},{18,... | collective-permute-start | bytes 294920 | tf_op jit(solution)/shard_map/ppermute | solution.py:297
  27.1 4.6 %collective-permute-start.9 = (f32[192,128]{1,0:T(8,128)S(1)}, f32[192,128]{1,0:T(8,128)S(1)}, u32[]{:S(2)}, u32[]{:S(2)}) collective-permute-start(f32[192,128]{1,0:T(8,128)S(1)} %get-tuple-element.73), channel_id=1, source_target_pairs={{1,2},{3,4},{5,6},{9,10},{11,12},{13,14},{17,18},{19,20},{21,22},{... | collective-permute-start | bytes 294920 | tf_op jit(solution)/shard_map/ppermute | solution.py:296
  38.0 11.0 %collective-permute-start.10 = (f32[8,192,128]{2,1,0:T(8,128)S(1)}, f32[8,192,128]{2,1,0:T(8,128)S(1)}, u32[]{:S(2)}, u32[]{:S(2)}) collective-permute-start(f32[8,192,128]{2,1,0:T(8,128)S(1)} %get-tuple-element.75.cur.prev), channel_id=1, source_target_pairs={{0,8},{1,9},{2,10},{3,11},{4,12},{5,13},{6,14},{7,15},{16,24},{17,... | collective-permute-start | bytes 2359304 | tf_op jit(solution)/shard_map/ppermute | solution.py:298
  38.1 10.9 %collective-permute-start.12 = (f32[4,192,128]{2,1,0:T(8,128)S(1)}, f32[4,192,128]{2,1,0:T(8,128)S(1)}, u32[]{:S(2)}, u32[]{:S(2)}) collective-permute-start(f32[4,192,128]{2,1,0:T(8,128)S(1)} %get-tuple-element.74.done), channel_id=1, source_target_pairs={{8,16},{9,17},{10,18},{11,19},{12,20},{13,21},{14,22},{15,23},{24,... | collective-permute-start | bytes 1179656 | tf_op jit(solution)/shard_map/ppermute | solution.py:289
  42.4 10.8 %collective-permute-start.11 = (f32[4,192,128]{2,1,0:T(8,128)S(1)}, f32[4,192,128]{2,1,0:T(8,128)S(1)}, u32[]{:S(2)}, u32[]{:S(2)}) collective-permute-start(f32[4,192,128]{2,1,0:T(8,128)S(1)} %get-tuple-element.76), channel_id=1, source_target_pairs={{8,16},{9,17},{10,18},{11,19},{12,20},{13,21},{14,22},{15,23},{24,... | collective-permute-start | bytes 1179656 | tf_op jit(solution)/shard_map/ppermute | solution.py:295
  43.5 4.6 %collective-permute-start.13 = (f32[192,128]{1,0:T(8,128)S(1)}, f32[192,128]{1,0:T(8,128)S(1)}, u32[]{:S(2)}, u32[]{:S(2)}) collective-permute-start(f32[192,128]{1,0:T(8,128)S(1)} %get-tuple-element.77), channel_id=1, source_target_pairs={{0,1},{2,3},{4,5},{6,7},{8,9},{10,11},{12,13},{14,15},{16,17},{18,... | collective-permute-start | bytes 294920 | tf_op jit(solution)/shard_map/ppermute | solution.py:297
  43.5 4.6 %collective-permute-start.14 = (f32[192,128]{1,0:T(8,128)S(1)}, f32[192,128]{1,0:T(8,128)S(1)}, u32[]{:S(2)}, u32[]{:S(2)}) collective-permute-start(f32[192,128]{1,0:T(8,128)S(1)} %get-tuple-element.78), channel_id=1, source_target_pairs={{1,2},{3,4},{5,6},{9,10},{11,12},{13,14},{17,18},{19,20},{21,22},{... | collective-permute-start | bytes 294920 | tf_op jit(solution)/shard_map/ppermute | solution.py:296
  53.3 11.0 %collective-permute-start.15 = (f32[8,192,128]{2,1,0:T(8,128)S(1)}, f32[8,192,128]{2,1,0:T(8,128)S(1)}, u32[]{:S(2)}, u32[]{:S(2)}) collective-permute-start(f32[8,192,128]{2,1,0:T(8,128)S(1)} %get-tuple-element.80.cur.prev), channel_id=1, source_target_pairs={{0,8},{1,9},{2,10},{3,11},{4,12},{5,13},{6,14},{7,15},{16,24},{17,... | collective-permute-start | bytes 2359304 | tf_op jit(solution)/shard_map/ppermute | solution.py:298
  53.4 10.9 %collective-permute-start.17 = (f32[4,192,128]{2,1,0:T(8,128)S(1)}, f32[4,192,128]{2,1,0:T(8,128)S(1)}, u32[]{:S(2)}, u32[]{:S(2)}) collective-permute-start(f32[4,192,128]{2,1,0:T(8,128)S(1)} %get-tuple-element.79.done), channel_id=1, source_target_pairs={{8,16},{9,17},{10,18},{11,19},{12,20},{13,21},{14,22},{15,23},{24,... | collective-permute-start | bytes 1179656 | tf_op jit(solution)/shard_map/ppermute | solution.py:289
  57.7 10.8 %collective-permute-start.16 = (f32[4,192,128]{2,1,0:T(8,128)S(1)}, f32[4,192,128]{2,1,0:T(8,128)S(1)}, u32[]{:S(2)}, u32[]{:S(2)}) collective-permute-start(f32[4,192,128]{2,1,0:T(8,128)S(1)} %get-tuple-element.81), channel_id=1, source_target_pairs={{8,16},{9,17},{10,18},{11,19},{12,20},{13,21},{14,22},{15,23},{24,... | collective-permute-start | bytes 1179656 | tf_op jit(solution)/shard_map/ppermute | solution.py:295
  58.9 4.6 %collective-permute-start.18 = (f32[192,128]{1,0:T(8,128)S(1)}, f32[192,128]{1,0:T(8,128)S(1)}, u32[]{:S(2)}, u32[]{:S(2)}) collective-permute-start(f32[192,128]{1,0:T(8,128)S(1)} %get-tuple-element.82), channel_id=1, source_target_pairs={{0,1},{2,3},{4,5},{6,7},{8,9},{10,11},{12,13},{14,15},{16,17},{18,... | collective-permute-start | bytes 294920 | tf_op jit(solution)/shard_map/ppermute | solution.py:297
  58.9 4.6 %collective-permute-start.19 = (f32[192,128]{1,0:T(8,128)S(1)}, f32[192,128]{1,0:T(8,128)S(1)}, u32[]{:S(2)}, u32[]{:S(2)}) collective-permute-start(f32[192,128]{1,0:T(8,128)S(1)} %get-tuple-element.83), channel_id=1, source_target_pairs={{1,2},{3,4},{5,6},{9,10},{11,12},{13,14},{17,18},{19,20},{21,22},{... | collective-permute-start | bytes 294920 | tf_op jit(solution)/shard_map/ppermute | solution.py:296
  68.7 11.2 %collective-permute-start.20 = (f32[8,192,128]{2,1,0:T(8,128)S(1)}, f32[8,192,128]{2,1,0:T(8,128)S(1)}, u32[]{:S(2)}, u32[]{:S(2)}) collective-permute-start(f32[8,192,128]{2,1,0:T(8,128)S(1)} %get-tuple-element.85.cur.prev), channel_id=1, source_target_pairs={{0,8},{1,9},{2,10},{3,11},{4,12},{5,13},{6,14},{7,15},{16,24},{17,... | collective-permute-start | bytes 2359304 | tf_op jit(solution)/shard_map/ppermute | solution.py:298
  68.8 11.1 %collective-permute-start.22 = (f32[4,192,128]{2,1,0:T(8,128)S(1)}, f32[4,192,128]{2,1,0:T(8,128)S(1)}, u32[]{:S(2)}, u32[]{:S(2)}) collective-permute-start(f32[4,192,128]{2,1,0:T(8,128)S(1)} %get-tuple-element.84.done), channel_id=1, source_target_pairs={{8,16},{9,17},{10,18},{11,19},{12,20},{13,21},{14,22},{15,23},{24,... | collective-permute-start | bytes 1179656 | tf_op jit(solution)/shard_map/ppermute | solution.py:289
  74.4 12.8 %collective-permute-start.21 = (f32[4,192,128]{2,1,0:T(8,128)S(1)}, f32[4,192,128]{2,1,0:T(8,128)S(1)}, u32[]{:S(2)}, u32[]{:S(2)}) collective-permute-start(f32[4,192,128]{2,1,0:T(8,128)S(1)} %get-tuple-element.86), channel_id=1, source_target_pairs={{8,16},{9,17},{10,18},{11,19},{12,20},{13,21},{14,22},{15,23},{24,... | collective-permute-start | bytes 1179656 | tf_op jit(solution)/shard_map/ppermute | solution.py:295
  87.4 11.5 %collective-permute-start.25 = (f32[8,192,128]{2,1,0:T(8,128)S(1)}, f32[8,192,128]{2,1,0:T(8,128)S(1)}, u32[]{:S(2)}, u32[]{:S(2)}) collective-permute-start(f32[8,192,128]{2,1,0:T(8,128)S(1)} %get-tuple-element.90.cur.prev), channel_id=1, source_target_pairs={{0,8},{1,9},{2,10},{3,11},{4,12},{5,13},{6,14},{7,15},{16,24},{17,... | collective-permute-start | bytes 2359304 | tf_op jit(solution)/shard_map/ppermute | solution.py:298
  87.5 11.4 %collective-permute-start.27 = (f32[4,192,128]{2,1,0:T(8,128)S(1)}, f32[4,192,128]{2,1,0:T(8,128)S(1)}, u32[]{:S(2)}, u32[]{:S(2)}) collective-permute-start(f32[4,192,128]{2,1,0:T(8,128)S(1)} %get-tuple-element.89.done), channel_id=1, source_target_pairs={{8,16},{9,17},{10,18},{11,19},{12,20},{13,21},{14,22},{15,23},{24,... | collective-permute-start | bytes 1179656 | tf_op jit(solution)/shard_map/ppermute | solution.py:289
  91.9 12.8 %collective-permute-start.26 = (f32[4,192,128]{2,1,0:T(8,128)S(1)}, f32[4,192,128]{2,1,0:T(8,128)S(1)}, u32[]{:S(2)}, u32[]{:S(2)}) collective-permute-start(f32[4,192,128]{2,1,0:T(8,128)S(1)} %get-tuple-element.91), channel_id=1, source_target_pairs={{8,16},{9,17},{10,18},{11,19},{12,20},{13,21},{14,22},{15,23},{24,... | collective-permute-start | bytes 1179656 | tf_op jit(solution)/shard_map/ppermute | solution.py:295
  92.9 4.6 %collective-permute-start.28 = (f32[192,128]{1,0:T(8,128)S(1)}, f32[192,128]{1,0:T(8,128)S(1)}, u32[]{:S(2)}, u32[]{:S(2)}) collective-permute-start(f32[192,128]{1,0:T(8,128)S(1)} %get-tuple-element.92), channel_id=1, source_target_pairs={{0,1},{2,3},{4,5},{6,7},{8,9},{10,11},{12,13},{14,15},{16,17},{18,... | collective-permute-start | bytes 294920 | tf_op jit(solution)/shard_map/ppermute | solution.py:297
  104.8 13.1 %collective-permute-start.30 = (f32[8,192,128]{2,1,0:T(8,128)S(1)}, f32[8,192,128]{2,1,0:T(8,128)S(1)}, u32[]{:S(2)}, u32[]{:S(2)}) collective-permute-start(f32[8,192,128]{2,1,0:T(8,128)S(1)} %get-tuple-element.95.cur.prev), channel_id=1, source_target_pairs={{0,8},{1,9},{2,10},{3,11},{4,12},{5,13},{6,14},{7,15},{16,24},{17,... | collective-permute-start | bytes 2359304 | tf_op jit(solution)/shard_map/ppermute | solution.py:298
  104.9 13.0 %collective-permute-start.32 = (f32[4,192,128]{2,1,0:T(8,128)S(1)}, f32[4,192,128]{2,1,0:T(8,128)S(1)}, u32[]{:S(2)}, u32[]{:S(2)}) collective-permute-start(f32[4,192,128]{2,1,0:T(8,128)S(1)} %get-tuple-element.94.done), channel_id=1, source_target_pairs={{8,16},{9,17},{10,18},{11,19},{12,20},{13,21},{14,22},{15,23},{24,... | collective-permute-start | bytes 1179656 | tf_op jit(solution)/shard_map/ppermute | solution.py:289
  108.9 13.3 %collective-permute-start.31 = (f32[4,192,128]{2,1,0:T(8,128)S(1)}, f32[4,192,128]{2,1,0:T(8,128)S(1)}, u32[]{:S(2)}, u32[]{:S(2)}) collective-permute-start(f32[4,192,128]{2,1,0:T(8,128)S(1)} %get-tuple-element.96), channel_id=1, source_target_pairs={{8,16},{9,17},{10,18},{11,19},{12,20},{13,21},{14,22},{15,23},{24,... | collective-permute-start | bytes 1179656 | tf_op jit(solution)/shard_map/ppermute | solution.py:295
  122.3 15.2 %collective-permute-start.35 = (f32[8,192,128]{2,1,0:T(8,128)S(1)}, f32[8,192,128]{2,1,0:T(8,128)S(1)}, u32[]{:S(2)}, u32[]{:S(2)}) collective-permute-start(f32[8,192,128]{2,1,0:T(8,128)S(1)} %get-tuple-element.100.wave.cur), channel_id=1, source_target_pairs={{0,8},{1,9},{2,10},{3,11},{4,12},{5,13},{6,14},{7,15},{16,24},{17,... | collective-permute-start | bytes 2359304 | tf_op jit(solution)/shard_map/ppermute | solution.py:298
  122.4 10.9 %collective-permute-start.37 = (f32[4,192,128]{2,1,0:T(8,128)S(1)}, f32[4,192,128]{2,1,0:T(8,128)S(1)}, u32[]{:S(2)}, u32[]{:S(2)}) collective-permute-start(f32[4,192,128]{2,1,0:T(8,128)S(1)} %get-tuple-element.101), channel_id=1, source_target_pairs={{8,16},{9,17},{10,18},{11,19},{12,20},{13,21},{14,22},{15,23},{24,... | collective-permute-start | bytes 1179656 | tf_op jit(solution)/shard_map/ppermute | solution.py:295
  124.2 13.3 %collective-permute-start.36 = (f32[4,192,128]{2,1,0:T(8,128)S(1)}, f32[4,192,128]{2,1,0:T(8,128)S(1)}, u32[]{:S(2)}, u32[]{:S(2)}) collective-permute-start(f32[4,192,128]{2,1,0:T(8,128)S(1)} %get-tuple-element.99.done), channel_id=1, source_target_pairs={{8,16},{9,17},{10,18},{11,19},{12,20},{13,21},{14,22},{15,23},{24,... | collective-permute-start | bytes 1179656 | tf_op jit(solution)/shard_map/ppermute | solution.py:289
  (14 other events, 65.1 us)
